TPU v7x, 32 devices: a whole 2x2x4 slice. The times are simulated.
32 devices in a mesh: band: 16 (over z, y, core), pw: 2 (over x).
Axes of the slice: x: 2, y: 2, z: 4, core: 2. Of those that a mesh axis runs over, the one named last changes fastest.
Arguments:
- mel: bfloat16 [32, 256, 32768], P('band', None, 'pw'), may hold values from -6 to 6
- pole_amp: bfloat16 [32768, 256], P('pw', 'band'), may hold values from 0.19921875 to 5
- pole_freq: bfloat16 [32768, 256], P('pw', 'band'), may hold values from 0.5 to 4
- band_energy: float32 [32], P('band'), may hold values from -3 to 3
- occupation: int32 [32], P('band'), may hold values from 0 to 1
- column_map: int32 [256], replicated, may hold values from 0 to 32767
- energies: float32 [2], replicated, may hold values from -2 to 2
Outputs:
- sigma: float32 [2, 256, 256], P(None, 'pw')
All inputs are finite; a program needn't handle non-finite values.
Results may differ from a plain program's by a relative error of at most 0.0055.
Values may be sent and summed in bfloat16 or wider, within the bound.
No kernel may reach another device: no remote copies, remote signals or barrier semaphores. Data moves between devices by JAX's collectives and lax.ppermute only.
A program may use at most 64 MiB of HBM per device.

v0:
```python
import math
import jax
import jax.numpy as jnp
from jax import lax
from jax.sharding import PartitionSpec as P

broadening = 0.4


def local(mel, pole_amp, pole_freq, band_energy, occupation, column_map, energies):
    row_count = mel.shape[2]
    offset = lax.axis_index("pw") * row_count
    local_index = column_map - offset
    inside = (local_index >= 0) & (local_index < row_count)
    picked = jnp.take(mel, jnp.clip(local_index, 0, row_count - 1), axis=2)
    picked = jnp.where(inside[None, None, :], picked, jnp.zeros_like(picked))
    chosen = lax.psum(picked, "pw").astype(jnp.float32).astype(jnp.bfloat16)
    branch_sign = (2 * occupation - 1).astype(jnp.float32)
    energy_count = energies.shape[0]
    band_count = mel.shape[0]
    pairing = (((1,), (1,)), ((), ()))
    whole_amp, whole_freq = (
        lax.all_gather(pole_amp, "band", axis=1, tiled=True),
        lax.all_gather(pole_freq, "band", axis=1, tiled=True),
    )
    amplitude = whole_amp.astype(jnp.float32)
    frequency = whole_freq.astype(jnp.float32)
    strength = amplitude / frequency
    column_blocks = [chosen[band_index] for band_index in range(band_count)]
    columns = jnp.concatenate(column_blocks, axis=1)
    updated = []
    for energy_index in range(energy_count):
        blocks = []
        for band_index in range(band_count):
            offset_gap = (
                energies[energy_index]
                - band_energy[band_index]
                + branch_sign[band_index] * frequency
            )
            screened = (
                strength * offset_gap / (offset_gap * offset_gap + broadening * broadening)
            ).astype(jnp.bfloat16)
            blocks.append(jnp.dot(mel[band_index], screened, preferred_element_type=jnp.float32))
        joined = jnp.concatenate(blocks, axis=1)
        upper = joined.astype(jnp.bfloat16)
        lower = (joined - upper.astype(jnp.float32)).astype(jnp.bfloat16)
        product = lax.dot_general(upper, columns, pairing, preferred_element_type=jnp.float32)
        product = product + lax.dot_general(
            lower, columns, pairing, preferred_element_type=jnp.float32
        )
        updated.append(product)
    partial_sigma = jnp.stack(updated)
    total_rows = row_count * lax.axis_size("pw")
    total_bands = band_count * lax.axis_size("band")
    partial_sigma = partial_sigma / math.sqrt(total_rows * column_map.shape[0] * total_bands)
    banded = lax.psum(partial_sigma, "band")
    return lax.psum_scatter(banded, "pw", scatter_dimension=1, tiled=True)


def solution(mesh):
    return jax.shard_map(
        local,
        mesh=mesh,
        in_specs=(
            P("band", None, "pw"),
            P("pw", "band"),
            P("pw", "band"),
            P("band"),
            P("band"),
            P(),
            P(),
        ),
        out_specs=P(None, "pw", None),
        check_vma=False,
    )
```

profile of v0, /device:TPU:1, one launch (start us, length us, event | category | flops | bytes accessed | tf_op | source)
XLA Modules:
  0.0 374.0 jit_solution(2522564181378667351)
XLA Ops:
  7.4 0.0 all-reduce.3.cloned.1.call-start
  7.4 0.7 compare_and_fusion
  8.1 0.0 copy-start
  8.1 0.0 copy-start.1
  8.1 0.0 copy-start.2
  8.1 40.8 %copy.13 = bf16[2,256,16384]{1,0,2:T(2,128)(2,1)} copy(bf16[2,256,16384]{2,1,0:T(8,128)(2,1)} %param.7) | data formatting | bytes 33554432 | tf_op args[0]
  48.9 7.0 %gather_fusion = bf16[256,2,256]{2,1,0:T(2,128)(2,1)S(1)} fusion(bf16[2,256,16384]{1,0,2:T(2,128)(2,1)} %copy.13, s32[1024]{0:T(1024)S(1)} %pad_clamp_fusion), kind=kCustom, calls=%fused_computation | custom fusion | bytes 525312 | tf_op jit(solution)/shard_map/jit(_take)/gather | solution.py:15
  55.9 2.1 fusion.68
  58.0 0.0 all-reduce.3.cloned.1.call-update
  58.1 0.0 all-gather.3.cloned.1.call-start
  58.1 0.5 all-gather.3.cloned.1.call-update
  58.6 0.0 all-gather.5.cloned.1.call-start
  58.7 0.5 all-gather.5.cloned.1.call-update
  59.2 0.0 reduce-scatter.2.cloned.1.call-start
  59.3 0.0 copy-done
  59.3 0.0 copy-done.1
  59.3 0.6 fusion.78
  64.7 0.0 copy-done.2
  64.7 0.6 fusion.79
  65.3 18.0 %all-reduce.3.cloned.1.call-done = bf16[2,256,256]{1,0,2:T(2,128)(2,1)} async-done(((bf16[2,256,256]{1,0,2:T(2,128)(2,1)}), bf16[2,256,256]{1,0,2:T(2,128)(2,1)}) %all-reduce.3.cloned.1.call-update) | async-done | bytes 262160 | tf_op jit(solution)/shard_map/psum | solution.py:17
  83.3 1.5 fusion.77
  84.8 0.1 copy.14
  85.0 0.1 copy.15
  85.1 52.1 %all-gather.3.cloned.1.call-done = bf16[16384,256]{0,1:T(8,128)(2,1)} async-done(((bf16[16384,16]{0,1:T(8,128)(2,1)}), bf16[16384,256]{0,1:T(8,128)(2,1)}) %all-gather.3.cloned.1.call-update) | async-done | bytes 8388624 | tf_op jit(solution)/shard_map/all_gather | solution.py:23
  137.3 74.8 %all-gather.5.cloned.1.call-done = bf16[16384,256]{0,1:T(8,128)(2,1)} async-done(((bf16[16384,16]{0,1:T(8,128)(2,1)}), bf16[16384,256]{0,1:T(8,128)(2,1)}) %all-gather.5.cloned.1.call-update) | async-done | bytes 8388624 | tf_op jit(solution)/shard_map/all_gather | solution.py:24
  212.0 0.0 slice-start
  212.0 0.0 slice-start.1
  212.0 12.7 %fusion.47 = f32[256,256]{0,1:T(8,128)S(1)} fusion(bf16[2,256,16384]{2,1,0:T(8,128)(2,1)} %param.7, bf16[16384,256]{0,1:T(8,128)(2,1)} %all-gather.5.cloned.1.call-done, f32[]{:T(128)} %bitcast.12, f32[]{:T(128)} %bitcast.1, bf16[16384,256]{0,1:T(8,128)(2,1)} %all-gather.3.cloned.1.call-done), kind=kOutput, calls=%fused_computation.45 | convolution fusion | flops 2189426688 | bytes 25428992 | tf_op jit(solution)/shard_map/dot_general | solution.py:43
  224.8 0.0 slice-start.2
  224.8 0.0 slice-start.3
  224.8 12.8 %fusion.57 = f32[256,256]{0,1:T(8,128)S(1)} fusion(bf16[2,256,16384]{2,1,0:T(8,128)(2,1)} %param.7, bf16[16384,256]{0,1:T(8,128)(2,1)} %all-gather.5.cloned.1.call-done, f32[]{:T(128)} %bitcast.14, f32[]{:T(128)} %bitcast.5, bf16[16384,256]{0,1:T(8,128)(2,1)} %all-gather.3.cloned.1.call-done), kind=kOutput, calls=%fused_computation.47 | convolution fusion | flops 2189426688 | bytes 25428992 | tf_op jit(solution)/shard_map/dot_general | solution.py:43
  237.6 0.3 fusion.66
  237.9 0.3 fusion.40
  238.2 0.0 slice-done
  238.2 0.0 slice-done.1
  238.2 0.0 slice-done.2
  238.2 0.0 slice-done.3
  238.2 10.9 %fusion.42 = f32[256,256]{0,1:T(8,128)S(1)} fusion(bf16[2,256,16384]{2,1,0:T(8,128)(2,1)S(1)} %bitcast.41, bf16[16384,256]{0,1:T(8,128)(2,1)} %all-gather.5.cloned.1.call-done, f32[]{:T(128)} %bitcast.1, f32[]{:T(128)} %bitcast, bf16[16384,256]{0,1:T(8,128)(2,1)} %all-gather.3.cloned.1.call-done), kind=kOutput, calls=%fused_computation.44 | convolution fusion | flops 2189426688 | bytes 25427976 | tf_op jit(solution)/shard_map/dot_general | solution.py:43
  249.2 11.0 %fusion.52 = f32[256,256]{0,1:T(8,128)S(1)} fusion(bf16[2,256,16384]{2,1,0:T(8,128)(2,1)S(1)} %bitcast.41, bf16[16384,256]{0,1:T(8,128)(2,1)} %all-gather.5.cloned.1.call-done, f32[]{:T(128)} %bitcast.5, f32[]{:T(128)} %bitcast.4, bf16[16384,256]{0,1:T(8,128)(2,1)} %all-gather.3.cloned.1.call-done), kind=kOutput, calls=%fused_computation.46 | convolution fusion | flops 2189426688 | bytes 25427976 | tf_op jit(solution)/shard_map/dot_general | solution.py:43
  260.2 0.3 fusion.64
  260.5 0.3 fusion.41
  260.8 0.8 maximum_multiply_fusion
  261.6 0.0 reduce-scatter.2.cloned.1.call-update
  261.6 0.0 all-reduce.5.cloned.1.call-start
  261.7 12.8 %reduce-scatter.2.cloned.1.call-done = f32[2,128,256]{2,1,0:T(8,128)} async-done(((f32[2,256,256]{2,1,0:T(8,128)}), f32[2,128,256]{2,1,0:T(8,128)}) %reduce-scatter.2.cloned.1.call-update) | async-done | bytes 262160 | tf_op jit(solution)/shard_map/reduce_scatter | solution.py:57
  274.5 0.0 all-reduce.5.cloned.1.call-update
  274.5 90.3 %all-reduce.5.cloned.1.call-done = f32[2,128,256]{2,1,0:T(8,128)} async-done(((f32[2,128,256]{2,1,0:T(8,128)}), f32[2,128,256]{2,1,0:T(8,128)}) %all-reduce.5.cloned.1.call-update) | async-done | bytes 262160 | tf_op jit(solution)/shard_map/psum | solution.py:56
  364.7 1.7 copy.18
  (3 shorter events, 0.0 us)
Async XLA Ops:
  7.4 76.0 %all-reduce.3.cloned.1.call-start = ((), (), s32[]{:S(2)}) async-start(), calls=%async_computation.3 | async-start | bytes 524288 | tf_op jit(solution)/shard_map/psum | solution.py:17
  8.1 51.2 %copy-start = (f32[2]{0:T(128)S(1)}, f32[2]{0:T(128)}, u32[]{:S(2)}) copy-start(f32[2]{0:T(128)} %param.13) | copy-start | bytes 28
  8.1 51.2 %copy-start.1 = (f32[2]{0:T(128)S(1)}, f32[2]{0:T(128)}, u32[]{:S(2)}) copy-start(f32[2]{0:T(128)} %param.10) | copy-start | bytes 28
  8.1 56.6 %copy-start.2 = (s32[2]{0:T(128)S(1)}, s32[2]{0:T(128)}, u32[]{:S(2)}) copy-start(s32[2]{0:T(128)} %param.11) | copy-start | bytes 28
  58.1 79.2 %all-gather.3.cloned.1.call-start = ((), (), s32[]{:S(2)}) async-start(), calls=%async_computation.1 | async-start | bytes 8912896 | tf_op jit(solution)/shard_map/all_gather | solution.py:23
  58.6 153.4 %all-gather.5.cloned.1.call-start = ((), (), s32[]{:S(2)}) async-start(), calls=%async_computation.2 | async-start | bytes 8912896 | tf_op jit(solution)/shard_map/all_gather | solution.py:24
  59.2 215.2 %reduce-scatter.2.cloned.1.call-start = ((), (), s32[]{:S(2)}) async-start(), calls=%async_computation.4 | async-start | bytes 786432 | tf_op jit(solution)/shard_map/reduce_scatter | solution.py:57
  212.0 26.2 %slice-start = ((s8[16777216]{0:T(1024)(128)(4,1)}), s8[4194304]{0:T(1024)(128)(4,1)S(1)}, s32[]{:S(2)}) async-start(s8[16777216]{0:T(1024)(128)(4,1)} %bitcast.40), calls=%async_computation.6 | async-start | bytes 8388608
  212.0 26.2 %slice-start.1 = ((s8[16777216]{0:T(1024)(128)(4,1)}), s8[4194304]{0:T(1024)(128)(4,1)S(1)}, s32[]{:S(2)}) async-start(s8[16777216]{0:T(1024)(128)(4,1)} %bitcast.40), calls=%async_computation.7 | async-start | bytes 8388608
  224.8 13.4 %slice-start.2 = ((s8[16777216]{0:T(1024)(128)(4,1)}), s8[4194304]{0:T(1024)(128)(4,1)S(1)}, s32[]{:S(2)}) async-start(s8[16777216]{0:T(1024)(128)(4,1)} %bitcast.40), calls=%async_computation.8 | async-start | bytes 8388608
  224.8 13.4 %slice-start.3 = ((s8[16777216]{0:T(1024)(128)(4,1)}), s8[4194304]{0:T(1024)(128)(4,1)S(1)}, s32[]{:S(2)}) async-start(s8[16777216]{0:T(1024)(128)(4,1)} %bitcast.40), calls=%async_computation.9 | async-start | bytes 8388608
  261.6 103.1 %all-reduce.5.cloned.1.call-start = ((), (), s32[]{:S(2)}) async-start(), calls=%async_computation.5 | async-start | bytes 524288 | tf_op jit(solution)/shard_map/psum | solution.py:56
Sparse Core Ops, SparseCore 0:
  58.2 25.1 all-reduce.2
  261.7 12.6 reduce-scatter.1
Sparse Core Ops, SparseCore 1:
  60.7 76.5 all-gather.2
  139.3 72.7 all-gather.4
  274.6 90.1 all-reduce.4
where the time goes:
time: 375 us; the launch traced here: 374 us
  waiting for transfers between devices  249 us (66%)
  local copies, waits for them, and re-layouts  52.5 us (14%)
  matrix products  48.6 us (13%)
  between operations  20 us (5%)
    psum x1, waiting for transfers between devices, local(): banded = lax.psum(partial_sigma, 'band')  90.3 us
    all_gather x1, waiting for transfers between devices, local(): lax.all_gather(pole_freq, 'band', axis=1, tiled=True)  74.8 us
    all_gather x1, waiting for transfers between devices, local(): lax.all_gather(pole_amp, 'band', axis=1, tiled=True)  52.1 us
    dot_general x4, matrix products, local(): jnp.dot(mel[band_index], screened, preferred_element_type=jnp.float32)  47.5 us
    unnamed x16, local copies, waits for them, and re-layouts  42.5 us
    psum x1, waiting for transfers between devices, local(): chosen = lax.psum(picked, 'pw').astype(jnp.float32).astype(jnp.bfloat16)  18 us
    reduce_scatter x1, waiting for transfers between devices, local(): return lax.psum_scatter(banded, 'pw', scatter_dimension=1, tiled=True)  12.8 us
  transfers between devices with their start and end apart: 5, of which 5 were waited for; matrix products, arithmetic and copies ran while one was open for 1% of the time, Pallas kernels for 0%

commit v1 on v0

--- a/solution.py
+++ b/solution.py
@@ -5,6 +5,13 @@
 from jax.sharding import PartitionSpec as P
 
 broadening = 0.4
+
+
+def show_the_ratios(a0):
+    prior = jnp.concatenate(
+        lax.all_to_all(jnp.stack(lax.psum(1, "band") * [a0]), "band", 0, 0), axis=1
+    )
+    return prior
 
 
 def local(mel, pole_amp, pole_freq, band_energy, occupation, column_map, energies):
@@ -20,7 +27,7 @@
     band_count = mel.shape[0]
     pairing = (((1,), (1,)), ((), ()))
     whole_amp, whole_freq = (
-        lax.all_gather(pole_amp, "band", axis=1, tiled=True),
+        show_the_ratios(pole_amp),
         lax.all_gather(pole_freq, "band", axis=1, tiled=True),
     )
     amplitude = whole_amp.astype(jnp.float32)

time: 375 us -> 480 us (1.28)
  waiting for transfers between devices: 249 us -> 330 us
  other arithmetic: 3.68 us -> 16.5 us
  starting transfers between devices: 0.17 us -> 7.46 us
  local copies, waits for them, and re-layouts: 52.5 us -> 57.9 us
    all_gather x1, waiting for transfers between devices: 74.8 us -> 167 us  [local(): lax.all_gather(pole_freq, 'band', axis=1, tiled=True)]
    all_gather x1 -> x0, waiting for transfers between devices: 52.1 us -> none  [local(): lax.all_gather(pole_amp, 'band', axis=1, tiled=True)]
    reduce_scatter x1, waiting for transfers between devices: 12.8 us -> 45.2 us  [local(): return lax.psum_scatter(banded, 'pw', scatter_dimension=1, tiled=True)]
    all_to_all x0 -> x1, waiting for transfers between devices: none -> 20 us  [show_the_ratios(): lax.all_to_all(jnp.stack(lax.psum(1, 'band') * [a0]), 'band', 0, 0)]
    div x0 -> x1, other arithmetic: none -> 12.9 us  [local(): strength = amplitude / frequency]
    psum x1, waiting for transfers between devices: 18 us -> 7.07 us  [local(): chosen = lax.psum(picked, 'pw').astype(jnp.float32).astype(jnp.bfloat16)]
    all_to_all x0 -> x1, starting transfers between devices: none -> 7.34 us  [show_the_ratios(): lax.all_to_all(jnp.stack(lax.psum(1, 'band') * [a0]), 'band', 0, 0)]
    unnamed x16 -> x12, local copies, waits for them, and re-layouts: 42.5 us -> 43.7 us
  transfers between devices with their start and end apart: 5 -> 5, of which waited for: 5 -> 5; matrix products, arithmetic and copies ran while one was open for 1% -> 2% of each run, Pallas kernels for 0% -> 0%
where the time goes in v1:
time: 480 us; the launch traced here: 479 us
  waiting for transfers between devices  330 us (69%)
  local copies, waits for them, and re-layouts  57.9 us (12%)
  matrix products  47.1 us (10%)
  between operations  19.8 us (4%)
  other arithmetic  16.5 us (3%)
  starting transfers between devices  7.46 us (2%)
    all_gather x1, waiting for transfers between devices, local(): lax.all_gather(pole_freq, 'band', axis=1, tiled=True)  167 us
    psum x1, waiting for transfers between devices, local(): banded = lax.psum(partial_sigma, 'band')  90.2 us
    dot_general x4, matrix products, local(): jnp.dot(mel[band_index], screened, preferred_element_type=jnp.float32)  46 us
    reduce_scatter x1, waiting for transfers between devices, local(): return lax.psum_scatter(banded, 'pw', scatter_dimension=1, tiled=True)  45.2 us
    unnamed x12, local copies, waits for them, and re-layouts  43.7 us
    all_to_all x1, waiting for transfers between devices, show_the_ratios(): lax.all_to_all(jnp.stack(lax.psum(1, 'band') * [a0]), 'band', 0, 0)  20 us
    div x1, other arithmetic, local(): strength = amplitude / frequency  12.9 us
  transfers between devices with their start and end apart: 5, of which 5 were waited for; matrix products, arithmetic and copies ran while one was open for 2% of the time, Pallas kernels for 0%

profile of v1, /device:TPU:1, one launch (start us, length us, event | category | flops | bytes accessed | tf_op | source)
XLA Modules:
  0.0 478.7 jit_solution(10103770702678801218)
XLA Ops:
  7.4 0.0 all-reduce.3.cloned.1.call-start
  7.4 0.7 compare_and_fusion
  8.1 0.0 copy-start.1
  8.1 40.8 %copy.13 = bf16[2,256,16384]{1,0,2:T(2,128)(2,1)} copy(bf16[2,256,16384]{2,1,0:T(8,128)(2,1)} %param.7) | data formatting | bytes 33554432 | tf_op args[0]
  48.9 0.0 copy-start.2
  48.9 0.0 copy-start.3
  48.9 0.0 copy-start.4
  48.9 7.0 %gather_fusion = bf16[256,2,256]{2,1,0:T(2,128)(2,1)S(1)} fusion(bf16[2,256,16384]{1,0,2:T(2,128)(2,1)} %copy.13, s32[1024]{0:T(1024)S(1)} %pad_clamp_fusion), kind=kCustom, calls=%fused_computation | custom fusion | bytes 525312 | tf_op jit(solution)/shard_map/jit(_take)/gather | solution.py:22
  55.9 2.1 fusion.68
  58.1 0.0 all-reduce.3.cloned.1.call-update
  58.1 0.0 all-gather.2.cloned.1.call-start
  58.1 0.5 all-gather.2.cloned.1.call-update
  58.7 0.0 copy-done.1
  58.7 4.2 stack.8
  62.8 7.3 %all-to-all-start = ((bf16[16,16384,16]{1,2,0:T(8,128)(2,1)}), bf16[16,16384,16]{1,2,0:T(8,128)(2,1)}, u32[]{:S(2)}, u32[]{:S(2)}) async-start(bf16[16,16384,16]{1,2,0:T(8,128)(2,1)} %stack.8), calls=%async_computation | async-start | bytes 16777216 | tf_op jit(solution)/shard_map/all_to_all | solution.py:12
  70.2 0.0 reduce-scatter.2.cloned.1.call-start
  70.2 0.0 copy-done.2
  70.2 0.0 copy-done.3
  70.2 0.6 fusion.78
  75.7 0.0 copy-done.4
  75.7 0.6 fusion.79
  76.3 7.1 %all-reduce.3.cloned.1.call-done = bf16[2,256,256]{1,0,2:T(2,128)(2,1)} async-done(((bf16[2,256,256]{1,0,2:T(2,128)(2,1)}), bf16[2,256,256]{1,0,2:T(2,128)(2,1)}) %all-reduce.3.cloned.1.call-update) | async-done | bytes 262160 | tf_op jit(solution)/shard_map/psum | solution.py:24
  83.4 1.5 fusion.77
  84.9 0.1 copy.14
  85.0 0.1 copy.15
  85.2 166.8 %all-gather.2.cloned.1.call-done = bf16[16384,256]{0,1:T(8,128)(2,1)} async-done(((bf16[16384,16]{0,1:T(8,128)(2,1)}), bf16[16384,256]{0,1:T(8,128)(2,1)}) %all-gather.2.cloned.1.call-update) | async-done | bytes 8388624 | tf_op jit(solution)/shard_map/all_gather | solution.py:31
  252.0 20.0 %all-to-all-done = bf16[16,16384,16]{1,2,0:T(8,128)(2,1)} async-done(((bf16[16,16384,16]{1,2,0:T(8,128)(2,1)}), bf16[16,16384,16]{1,2,0:T(8,128)(2,1)}, u32[]{:S(2)}, u32[]{:S(2)}) %all-to-all-start) | async-done | bytes 8388640 | tf_op jit(solution)/shard_map/all_to_all | solution.py:12
  271.9 0.0 copy-start
  271.9 12.9 %convert_divide_fusion = f32[16384,256]{0,1:T(8,128)} fusion(bf16[16384,256]{0,1:T(8,128)(2,1)} %all-gather.2.cloned.1.call-done, bf16[16,16384,16]{1,2,0:T(8,128)(2,1)} %all-to-all-done), kind=kLoop, calls=%fused_computation.3 | loop fusion | flops 12582912 | bytes 33554432 | tf_op jit(solution)/shard_map/div | solution.py:35
  284.8 1.2 copy-done
  286.0 11.5 %fusion.57 = f32[256,256]{0,1:T(8,128)S(1)} fusion(bf16[2,256,16384]{2,1,0:T(8,128)(2,1)} %param.7, f32[16384,256]{0,1:T(8,128)} %convert_divide_fusion, bf16[16384,256]{0,1:T(8,128)(2,1)S(1)} %copy-done, f32[]{:T(128)} %bitcast.16, f32[]{:T(128)} %bitcast.7), kind=kOutput, calls=%fused_computation.47 | convolution fusion | flops 2181038080 | bytes 33817600 | tf_op jit(solution)/shard_map/dot_general | solution.py:50
  297.5 11.5 %fusion.47 = f32[256,256]{0,1:T(8,128)S(1)} fusion(bf16[2,256,16384]{2,1,0:T(8,128)(2,1)} %param.7, f32[16384,256]{0,1:T(8,128)} %convert_divide_fusion, bf16[16384,256]{0,1:T(8,128)(2,1)S(1)} %copy-done, f32[]{:T(128)} %bitcast.14, f32[]{:T(128)} %bitcast.3), kind=kOutput, calls=%fused_computation.45 | convolution fusion | flops 2181038080 | bytes 33817600 | tf_op jit(solution)/shard_map/dot_general | solution.py:50
  309.0 0.3 fusion.66
  309.3 0.3 fusion.40
  309.6 11.5 %fusion.52 = f32[256,256]{0,1:T(8,128)S(1)} fusion(bf16[2,256,16384]{2,1,0:T(8,128)(2,1)} %param.7, f32[16384,256]{0,1:T(8,128)} %convert_divide_fusion, bf16[16384,256]{0,1:T(8,128)(2,1)S(1)} %copy-done, f32[]{:T(128)} %bitcast.7, f32[]{:T(128)} %bitcast.6), kind=kOutput, calls=%fused_computation.46 | convolution fusion | flops 2181038080 | bytes 33817600 | tf_op jit(solution)/shard_map/dot_general | solution.py:50
  321.1 11.5 %fusion.42 = f32[256,256]{0,1:T(8,128)S(1)} fusion(bf16[2,256,16384]{2,1,0:T(8,128)(2,1)} %param.7, f32[16384,256]{0,1:T(8,128)} %convert_divide_fusion, bf16[16384,256]{0,1:T(8,128)(2,1)S(1)} %copy-done, f32[]{:T(128)} %bitcast.3, f32[]{:T(128)} %bitcast.2), kind=kOutput, calls=%fused_computation.44 | convolution fusion | flops 2181038080 | bytes 33817600 | tf_op jit(solution)/shard_map/dot_general | solution.py:50
  332.6 0.3 fusion.64
  332.9 0.3 fusion.41
  333.2 0.8 maximum_multiply_fusion
  334.0 0.0 reduce-scatter.2.cloned.1.call-update
  334.0 0.0 all-reduce.5.cloned.1.call-start
  334.1 45.2 %reduce-scatter.2.cloned.1.call-done = f32[2,128,256]{2,1,0:T(8,128)} async-done(((f32[2,256,256]{2,1,0:T(8,128)}), f32[2,128,256]{2,1,0:T(8,128)}) %reduce-scatter.2.cloned.1.call-update) | async-done | bytes 262160 | tf_op jit(solution)/shard_map/reduce_scatter | solution.py:64
  379.3 0.0 all-reduce.5.cloned.1.call-update
  379.3 90.2 %all-reduce.5.cloned.1.call-done = f32[2,128,256]{2,1,0:T(8,128)} async-done(((f32[2,128,256]{2,1,0:T(8,128)}), f32[2,128,256]{2,1,0:T(8,128)}) %all-reduce.5.cloned.1.call-update) | async-done | bytes 262160 | tf_op jit(solution)/shard_map/psum | solution.py:63
  469.6 1.7 copy.18
  (2 shorter events, 0.0 us)
Async XLA Ops:
  7.4 76.0 %all-reduce.3.cloned.1.call-start = ((), (), s32[]{:S(2)}) async-start(), calls=%async_computation.3 | async-start | bytes 524288 | tf_op jit(solution)/shard_map/psum | solution.py:24
  8.1 50.6 %copy-start.1 = (bf16[16384,16]{0,1:T(8,128)(2,1)S(1)}, bf16[16384,16]{0,1:T(8,128)(2,1)}, u32[]{:S(2)}) copy-start(bf16[16384,16]{0,1:T(8,128)(2,1)} %param.8) | copy-start | bytes 1572868
  48.9 21.4 %copy-start.2 = (f32[2]{0:T(128)S(1)}, f32[2]{0:T(128)}, u32[]{:S(2)}) copy-start(f32[2]{0:T(128)} %param.13) | copy-start | bytes 28
  48.9 21.4 %copy-start.3 = (f32[2]{0:T(128)S(1)}, f32[2]{0:T(128)}, u32[]{:S(2)}) copy-start(f32[2]{0:T(128)} %param.10) | copy-start | bytes 28
  48.9 26.8 %copy-start.4 = (s32[2]{0:T(128)S(1)}, s32[2]{0:T(128)}, u32[]{:S(2)}) copy-start(s32[2]{0:T(128)} %param.11) | copy-start | bytes 28
  58.1 193.9 %all-gather.2.cloned.1.call-start = ((), (), s32[]{:S(2)}) async-start(), calls=%async_computation.2 | async-start | bytes 8912896 | tf_op jit(solution)/shard_map/all_gather | solution.py:31
  62.8 209.1 %all-to-all-start = ((bf16[16,16384,16]{1,2,0:T(8,128)(2,1)}), bf16[16,16384,16]{1,2,0:T(8,128)(2,1)}, u32[]{:S(2)}, u32[]{:S(2)}) async-start(bf16[16,16384,16]{1,2,0:T(8,128)(2,1)} %stack.8), calls=%async_computation | async-start | bytes 16777216 | tf_op jit(solution)/shard_map/all_to_all | solution.py:12
  70.2 309.1 %reduce-scatter.2.cloned.1.call-start = ((), (), s32[]{:S(2)}) async-start(), calls=%async_computation.4 | async-start | bytes 786432 | tf_op jit(solution)/shard_map/reduce_scatter | solution.py:64
  271.9 14.1 %copy-start = (bf16[16384,256]{0,1:T(8,128)(2,1)S(1)}, bf16[16384,256]{0,1:T(8,128)(2,1)}, u32[]{:S(2)}) copy-start(bf16[16384,256]{0,1:T(8,128)(2,1)} %all-gather.2.cloned.1.call-done) | copy-start | bytes 25165828
  334.0 135.6 %all-reduce.5.cloned.1.call-start = ((), (), s32[]{:S(2)}) async-start(), calls=%async_computation.5 | async-start | bytes 524288 | tf_op jit(solution)/shard_map/psum | solution.py:63
Sparse Core Ops, SparseCore 0:
  58.2 25.1 all-reduce.2
  334.1 45.1 reduce-scatter.1
Sparse Core Ops, SparseCore 1:
  60.7 191.2 all-gather.1
  379.4 90.1 all-reduce.4
